TPU v7x, 32 devices: a whole 2x2x4 slice. The times are simulated.
32 devices in a mesh: dirs: 2 (over y), taps: 4 (over z), tm: 2 (over x), floors: 2 (over core).
Axes of the slice: x: 2, y: 2, z: 4, core: 2. Of those that a mesh axis runs over, the one named last changes fastest.
Arguments:
- pressures: bfloat16 [4096, 16384], P(('dirs', 'tm'), ('taps', 'floors')), parts along dimension 0, may hold values from -6 to 6
- tap_area: bfloat16 [16384], P(('taps', 'floors')), may hold values from 0.29882812 to 3
- tap_panel: int32 [16384], P(('taps', 'floors')), may hold values from 0 to 255
- tap_floor: int32 [16384], P(('taps', 'floors')), may hold values from 0 to 15
- panel_shape: bfloat16 [256, 512], replicated, may hold values from -0.046875 to 0.046875
- floor_shape: bfloat16 [16, 512], replicated, may hold values from -0.25 to 0.25
- mode_order: int32 [512], replicated, may hold values from 0 to 511, each once
- mode_decay: float32 [512], replicated, may hold values from 4.8828125e-05 to 0.08
- mode_freq: float32 [512], replicated, may hold values from 0.02 to 1.2
Outputs:
- modal_response: float32 [512, 4096], P(('taps', 'floors'), ('dirs', 'tm')), parts along dimension 1
- floor_motion: float32 [16, 4096], P(('taps', 'floors'), ('dirs', 'tm')), parts along dimension 1
- floor_load: float32 [16, 4096], P(('taps', 'floors'), ('dirs', 'tm')), parts along dimension 1
There are 2 independent parts, one for each index of `dirs`. A program takes and returns all parts, laid end to end along the dimension named above; an argument that names none is the same for every part. Nothing has to cross between parts.
All inputs are finite; a program needn't handle non-finite values.
Results may differ from a plain program's by a relative error of at most 0.0029.
Values sent between devices are 32-bit elements; how exact they have to be, the bound alone decides.
A program may use at most 64 MiB of HBM per device.

v0:
```python
import jax
import jax.numpy as jnp
from jax import lax
from jax.sharding import PartitionSpec as P

BLK = 256


def on_device(
    pressures,
    tap_area,
    tap_panel,
    tap_floor,
    panel_shape,
    floor_shape,
    mode_order,
    mode_decay,
    mode_freq,
):
    highest = lax.Precision.HIGHEST
    modes = mode_order.shape[0]
    owners = lax.axis_size(("taps", "floors"))
    mode_dev = modes // owners
    time_dev = pressures.shape[0]
    tap_dev = pressures.shape[1]
    floor_count = floor_shape.shape[0]
    block_count = time_dev // BLK
    owner = lax.axis_index(("taps", "floors"))
    load_scale = (floor_count / (tap_dev * owners)) ** 0.5
    floor_ids = jnp.arange(floor_count, dtype=jnp.int32)
    weights = jnp.where(
        tap_floor[None, :] == floor_ids[:, None], tap_area[None, :], jnp.zeros((), jnp.bfloat16)
    )
    load_part = lax.dot_general(
        weights, pressures, (((1,), (1,)), ((), ())), preferred_element_type=jnp.float32
    )
    floor_load = lax.psum_scatter(load_part, ("taps", "floors"), scatter_dimension=0, tiled=True)
    ordered = jnp.take(panel_shape, mode_order, axis=1)
    tributary = (
        jnp.take(ordered, tap_panel, axis=0).astype(jnp.float32)
        * tap_area.astype(jnp.float32)[:, None]
    ).astype(jnp.bfloat16)
    forces = lax.psum_scatter(
        lax.dot_general(
            tributary, pressures, (((0,), (1,)), ((), ())), preferred_element_type=jnp.float32
        ),
        ("taps", "floors"),
        scatter_dimension=0,
        tiled=True,
    )
    local_order = lax.dynamic_slice_in_dim(mode_order, owner * mode_dev, mode_dev)
    decays = jnp.take(mode_decay, local_order)
    angles = jnp.take(mode_freq, local_order)
    input_gain = jnp.sqrt(-jnp.expm1(-2.0 * decays))
    steps_in = jnp.arange(BLK, dtype=jnp.float32)
    differ = steps_in[:, None] - steps_in[None, :]
    causal = differ >= 0.0
    distance = jnp.maximum(differ, 0.0)
    toeplitz = jnp.where(
        causal[None],
        input_gain[:, None, None]
        * jnp.exp(-decays[:, None, None] * distance)
        * jnp.cos(angles[:, None, None] * distance),
        0.0,
    )
    force_blocks = forces.reshape(mode_dev, block_count, BLK)
    zero_resp = jnp.einsum("mij,mbj->mbi", toeplitz, force_blocks, precision=highest)
    to_end = BLK - 1.0 - steps_in
    end_scale = input_gain[:, None] * jnp.exp(-decays[:, None] * to_end)
    end_re = end_scale * jnp.cos(angles[:, None] * to_end)
    end_im = end_scale * jnp.sin(angles[:, None] * to_end)
    ends_re = jnp.einsum("mj,mbj->mb", end_re, force_blocks, precision=highest)
    ends_im = jnp.einsum("mj,mbj->mb", end_im, force_blocks, precision=highest)
    count = float(BLK)
    scale = jnp.exp(-decays * count)
    blk_re = scale * jnp.cos(angles * count)
    blk_im = scale * jnp.sin(angles * count)

    def advance(carried, inputs):
        state_re, state_im = carried
        push_re, push_im = inputs
        next_re = blk_re * state_re - blk_im * state_im + push_re
        next_im = blk_im * state_re + blk_re * state_im + push_im
        return ((next_re, next_im), carried)

    zeros_state = jnp.zeros((mode_dev,), jnp.float32)
    (group_re, group_im), (enter_re, enter_im) = lax.scan(
        advance, (zeros_state, zeros_state), (ends_re.T, ends_im.T)
    )
    gathered_re, gathered_im = (
        lax.all_gather(group_re[None], "tm", axis=0, tiled=True),
        lax.all_gather(group_im[None], "tm", axis=0, tiled=True),
    )
    position = lax.axis_index("tm")
    sources = jnp.arange(gathered_re.shape[0], dtype=jnp.int32)
    distance_tm = position - 1 - sources
    earlier_mask = (distance_tm >= 0)[:, None]
    lengths = (jnp.maximum(distance_tm, 0).astype(jnp.float32) * time_dev)[:, None]
    decay_pw = jnp.exp(-decays[None, :] * lengths)
    pw_re = decay_pw * jnp.cos(angles[None, :] * lengths)
    pw_im = decay_pw * jnp.sin(angles[None, :] * lengths)
    in_re = jnp.sum(jnp.where(earlier_mask, pw_re * gathered_re - pw_im * gathered_im, 0.0), axis=0)
    in_im = jnp.sum(jnp.where(earlier_mask, pw_im * gathered_re + pw_re * gathered_im, 0.0), axis=0)
    block_start = (jnp.arange(block_count, dtype=jnp.float32) * BLK)[:, None]
    start_scale = jnp.exp(-decays[None, :] * block_start)
    pb_re = start_scale * jnp.cos(angles[None, :] * block_start)
    pb_im = start_scale * jnp.sin(angles[None, :] * block_start)
    yb_re = pb_re * in_re[None, :] - pb_im * in_im[None, :] + enter_re
    yb_im = pb_im * in_re[None, :] + pb_re * in_im[None, :] + enter_im
    ahead = steps_in + 1.0
    ahead_scale = jnp.exp(-decays[:, None] * ahead)
    fr_re = ahead_scale * jnp.cos(angles[:, None] * ahead)
    fr_im = ahead_scale * jnp.sin(angles[:, None] * ahead)
    free_part = fr_re[:, None, :] * yb_re.T[:, :, None] - fr_im[:, None, :] * yb_im.T[:, :, None]
    motion = (zero_resp + free_part).reshape(mode_dev, time_dev)
    local_shape = jnp.take(floor_shape, local_order, axis=1).astype(jnp.float32)
    motion_part = jnp.dot(
        local_shape, motion, precision=highest, preferred_element_type=jnp.float32
    )
    floor_motion = lax.psum_scatter(
        motion_part, ("taps", "floors"), scatter_dimension=0, tiled=True
    )
    return (motion, floor_motion, floor_load * load_scale)


def solution(mesh):
    in_specs = (
        P(("dirs", "tm"), ("taps", "floors")),
        P(("taps", "floors")),
        P(("taps", "floors")),
        P(("taps", "floors")),
        P(),
        P(),
        P(),
        P(),
        P(),
    )
    out_specs = (
        P(("taps", "floors"), ("dirs", "tm")),
        P(("taps", "floors"), ("dirs", "tm")),
        P(("taps", "floors"), ("dirs", "tm")),
    )
    return jax.shard_map(
        on_device, mesh=mesh, in_specs=in_specs, out_specs=out_specs, check_vma=False
    )
```

profile of v0, /device:TPU:3, one launch (start us, length us, event | category | flops | bytes accessed | tf_op | source)
XLA Modules:
  0.0 207.4 jit_solution(1603378108236540857)
XLA Ops:
  7.2 0.7 compare_select_fusion.1
  7.9 0.7 compare_and_fusion.2
  8.6 0.7 fusion.46
  9.3 0.7 compare_and_fusion
  10.0 0.7 convert_element_type.18
  10.7 1.1 copy.22
  11.8 2.0 gather_fusion
  14.0 7.5 %gather_fusion.1 = bf16[2048,512]{1,0:T(8,128)(2,1)S(1)} fusion(bf16[256,512]{1,0:T(8,128)(2,1)S(1)} %copy.23, s32[2048]{0:T(1024)S(1)} %fusion.46), kind=kCustom, calls=%fused_computation.3 | custom fusion | bytes 4202496 | tf_op jit(solution)/shard_map/jit(_take)/gather | solution.py:40
  21.7 6.5 %fusion.16 = f32[512,1024]{1,0:T(8,128)} fusion(bf16[1024,2048]{1,0:T(8,128)(2,1)} %param.13, f32[2048]{0:T(1024)S(1)} %convert_element_type.18, bf16[2048,512]{1,0:T(8,128)(2,1)S(1)} %gather_fusion.1, pred[2048]{0:T(1024)(128)(4,1)S(1)} %compare_and_fusion), kind=kOutput, calls=%fused_computation.26 | convolution fusion | flops 2151677952 | bytes 8398848 | tf_op jit(solution)/shard_map/dot_general | solution.py:44
  28.3 0.8 compare_and_fusion.1
  29.1 0.8 gather_fusion.3
  29.9 0.8 gather_fusion.4
  30.8 0.6 gather_fusion.2
  33.6 4.0 %fusion.33 = f32[16,1024]{1,0:T(8,128)} fusion(bf16[1024,2048]{1,0:T(8,128)(2,1)} %param.13, s32[2048]{0:T(1024)S(1)} %copy-done.5, bf16[2048]{0:T(1024)(128)(2,1)S(1)} %copy-done.3), kind=kOutput, calls=%fused_computation.48 | convolution fusion | flops 67174400 | bytes 4272128 | tf_op jit(solution)/shard_map/dot_general | solution.py:34
  37.6 25.0 %reduce-scatter.2.cloned.1.call-done = f32[64,1024]{1,0:T(8,128)} async-done(((f32[512,1024]{1,0:T(8,128)}), f32[64,1024]{1,0:T(8,128)}) %reduce-scatter.2.cloned.1.call-update) | async-done | bytes 262160 | tf_op jit(solution)/shard_map/reduce_scatter | solution.py:43
  62.6 1.1 reshape.184
  63.7 0.6 fusion.38
  64.4 0.6 fusion.36
  66.0 3.8 %all-reduce.5 = (f32[128]{0:T(128)S(1)}, f32[128]{0:T(128)S(1)}) all-reduce(f32[128]{0:T(128)S(1)} %dynamic-update-slice.1, f32[128]{0:T(128)S(1)} %dynamic-update-slice), channel_id=3, replica_groups=mesh['dirs'=2,'taps'=4,'tm'=2,'floors'=2] {'tm'}, use_global_device_ids=true, to_apply=%add.1 | all-reduce | flops 256 | bytes 2048
  70.3 70.5 %fusion.20 = f32[64,4,256]{2,1,0:T(4,128)S(1)} fusion(f32[64,4,256]{2,1,0:T(4,128)S(1)} %reshape.184, f32[64]{0:T(128)S(1)} %get-tuple-element.116, f32[256,256]{1,0:T(8,128)S(1)} %fusion.24, f32[64]{0:T(128)S(1)} %get-tuple-element.115, f32[64]{0:T(128)S(1)} %get-tuple-element.129, pred[256,256]{1,0:T(8,128)(4,1)S(1)} %fusion.25, f32[64,4]{1,0:T(8,128)S(1)} %copy.25, ...), kind=kOutput, calls=%fused_computation.30 | convolution fusion | flops 222560256 | bytes 985856 | tf_op jit(solution)/shard_map/mij,mbj->mbi/dot_general | solution.py:67
  141.0 0.9 fusion.42
  143.2 54.7 %all-reduce.8.cloned.1.call-done = (f32[16,1024]{1,0:T(8,128)}, f32[16,1024]{1,0:T(8,128)}) async-done(((f32[16,1024]{1,0:T(8,128)}, f32[16,1024]{1,0:T(8,128)}), (f32[16,1024]{1,0:T(8,128)}, f32[16,1024]{1,0:T(8,128)})) %all-reduce.8.cloned.1.call-update) | async-done | bytes 131088
  197.9 1.4 constant_dynamic-slice_fusion
  199.2 1.4 dynamic-slice_multiply_fusion
  (66 shorter events, 4.6 us)
Async XLA Ops:
  7.2 21.9 %copy-start = (f32[512]{0:T(512)S(1)}, f32[512]{0:T(512)}, u32[]{:S(2)}) copy-start(f32[512]{0:T(512)} %param.20) | copy-start | bytes 6148
  7.2 55.4 %reduce-scatter.2.cloned.1.call-start = ((), (), s32[]{:S(2)}) async-start(), calls=%async_computation.1 | async-start | bytes 2359296 | tf_op jit(solution)/shard_map/reduce_scatter | solution.py:43
  21.6 8.3 %copy-start.1 = (f32[512]{0:T(512)S(1)}, f32[512]{0:T(512)}, u32[]{:S(2)}) copy-start(f32[512]{0:T(512)} %param.21) | copy-start | bytes 6148
  21.6 9.1 %copy-start.4 = (bf16[16,512]{1,0:T(8,128)(2,1)S(1)}, bf16[16,512]{1,0:T(8,128)(2,1)}, u32[]{:S(2)}) copy-start(bf16[16,512]{1,0:T(8,128)(2,1)} %param.18) | copy-start | bytes 49156
  21.6 9.9 %copy-start.7 = (u32[32]{0:T(128)S(1)}, u32[32]{0:T(128)}, u32[]{:S(2)}) copy-start(u32[32]{0:T(128)} %constant.106) | copy-start | bytes 388
  21.6 11.9 %copy-start.3 = (bf16[2048]{0:T(1024)(128)(2,1)S(1)}, bf16[2048]{0:T(1024)(128)(2,1)}, u32[]{:S(2)}) copy-start(bf16[2048]{0:T(1024)(128)(2,1)} %param.14) | copy-start | bytes 12292
  21.6 11.9 %copy-start.5 = (s32[2048]{0:T(1024)S(1)}, s32[2048]{0:T(1024)}, u32[]{:S(2)}) copy-start(s32[2048]{0:T(1024)} %param.16) | copy-start | bytes 24580
  28.2 169.6 %all-reduce.8.cloned.1.call-start = ((), (), s32[]{:S(2)}) async-start(), calls=%async_computation.2 | async-start | bytes 262144
  70.3 71.6 %copy-start.6 = (u32[32]{0:T(128)S(1)}, u32[32]{0:T(128)}, u32[]{:S(2)}) copy-start(u32[32]{0:T(128)} %constant.118) | copy-start | bytes 388
  140.9 59.6 %copy-start.2 = (f32[8,8,4,256]{3,1,2,0:T(8,128)}, f32[8,8,4,256]{3,1,2,0:T(8,128)S(1)}, u32[]{:S(2)}) copy-start(f32[8,8,4,256]{3,1,2,0:T(8,128)S(1)} %copy.31) | copy-start | bytes 786436
Sparse Core Ops, SparseCore 0:
  28.3 34.2 reduce-scatter.1
  142.0 55.7 all-reduce.7
where the time goes:
time: 211 us; the launch traced here: 207 us
  matrix products  83.3 us (39%)
  waiting for transfers between devices  79.7 us (38%)
  local copies, waits for them, and re-layouts  18 us (9%)
  between operations  15.6 us (7%)
  other arithmetic  6.88 us (3%)
  blocking collectives  3.76 us (2%)
    dot_general x1, matrix products, on_device(): jnp.einsum('mij,mbj->mbi', toeplitz, force_blocks, precision=highest)  70.5 us
    unnamed x3, waiting for transfers between devices  54.7 us
    reduce_scatter x1, waiting for transfers between devices, on_device(): lax.psum_scatter(lax.dot_general(tributary, pressures, (((0,), (1,)), (()...  25 us
    gather x1, local copies, waits for them, and re-layouts, on_device(): jnp.take(ordered, tap_panel, axis=0).astype(jnp.float32)  7.54 us
    dot_general x1, matrix products, on_device(): lax.dot_general(tributary, pressures, (((0,), (1,)), ((), ())), preferred...  6.54 us
    unnamed x26, local copies, waits for them, and re-layouts  4.29 us
  transfers between devices with their start and end apart: 2, of which 2 were waited for; matrix products, arithmetic and copies ran while one was open for 4% of the time, Pallas kernels for 0%

commit v1 on v0

v1 whole, which is shorter than its diff:
```python
import functools

import jax
import jax.numpy as jnp
from jax import lax
from jax.experimental import pallas as pl
from jax.experimental.pallas import tpu as pltpu
from jax.sharding import PartitionSpec as P

MESH = pl.DeviceIdType.MESH
LANES = 128
LAG = 2
NT = (((1,), (1,)), ((), ()))


def dot_nt(a, b):
    return lax.dot_general(a, b, NT, preferred_element_type=jnp.float32)


def dot_split(a, b):
    hi = b.astype(jnp.bfloat16)
    lo = (b - hi.astype(jnp.float32)).astype(jnp.bfloat16)
    return jnp.dot(a, hi, preferred_element_type=jnp.float32) + jnp.dot(
        a, lo, preferred_element_type=jnp.float32
    )


def kernel(
    cfg,
    p_hbm, area_ref, panel_ref, floor_ref, shape_ref, fshape_ref, order_ref, decay_ref, freq_ref,
    y_ref, fm_ref, fl_ref,
    pv, w_ref, mine, send_p, recv_p, rin, lin, rout, lout, xs, fb, tabs, loc, st_send, st_recv,
    fs, fr,
    p_sem, pp_s, pp_r, r_s, r_r, l_s, l_r, x_s, x_r, t_s, t_r, f_s, f_r,
):
    nz, nc, ntm, splits = cfg
    owners = nz * nc
    z = lax.axis_index("taps")
    c = lax.axis_index("floors")
    x = lax.axis_index("tm")
    me = z * nc + c
    other = nc - 1 - c
    time_dev, taps = pv.shape
    panels, modes = shape_ref.shape
    floors = fshape_ref.shape[0]
    rows = panels + floors
    th = time_dev // nc
    tblocks = th // LANES
    crows = rows // splits
    nch = tblocks * splits
    md = modes // owners
    fd = floors // owners
    f32 = jnp.float32
    bf16 = jnp.bfloat16

    barrier = pltpu.get_barrier_semaphore()

    def greet(k, carry):
        j = lax.rem(me + k, owners)
        pl.semaphore_signal(
            barrier, inc=1, device_id={"taps": j // nc, "floors": lax.rem(j, nc)}, device_id_type=MESH
        )
        return carry

    lax.fori_loop(1, owners, greet, 0)
    for k in range(1, ntm):
        pl.semaphore_signal(
            barrier, inc=1, device_id={"tm": lax.rem(x + k, ntm)}, device_id_type=MESH
        )

    step_t = min(256, th)
    per_half = th // step_t
    loads = []
    for h in range(2):
        half = other if h == 0 else c
        for b in range(per_half):
            off = pl.multiple_of(half * th + b * step_t, step_t)
            cp = pltpu.make_async_copy(
                p_hbm.at[pl.ds(off, step_t)], pv.at[pl.ds(off, step_t)], p_sem.at[h * per_half + b]
            )
            cp.start()
            loads.append((cp, off))

    area = area_ref[...].astype(f32)
    ids = lax.broadcasted_iota(jnp.int32, (panels, taps), 0)
    w_ref[0:panels, :] = jnp.where(panel_ref[...] == ids, area, 0.0).astype(bf16)
    fids = lax.broadcasted_iota(jnp.int32, (floors, taps), 0)
    w_ref[panels:rows, :] = jnp.where(floor_ref[...] == fids, area, 0.0).astype(bf16)

    def sums(b, h, dst):
        cp, off = loads[h * per_half + b]
        cp.wait()
        q = dot_nt(w_ref[...], pv[pl.ds(off, step_t), :])
        for i in range(step_t // LANES):
            for s in range(splits):
                dst[(b * step_t // LANES + i) * splits + s] = q[
                    s * crows : (s + 1) * crows, i * LANES : (i + 1) * LANES
                ]

    def pair_copy(k):
        return pltpu.make_async_remote_copy(
            src_ref=send_p.at[k], dst_ref=recv_p.at[k], send_sem=pp_s.at[k], recv_sem=pp_r.at[k],
            device_id={"floors": other}, device_id_type=MESH,
        )

    per_step = step_t // LANES * splits
    for b in range(per_half):
        sums(b, 0, send_p)
        if b == 0:
            pl.semaphore_wait(barrier, owners - 1 + ntm - 1)
        for k in range(b * per_step, (b + 1) * per_step):
            pair_copy(k).start()
    for b in range(per_half):
        sums(b, 1, mine)

    @pl.when(z == 0)
    def _():
        rin[...] = jnp.zeros_like(rin)

    @pl.when(z == nz - 1)
    def _():
        lin[...] = jnp.zeros_like(lin)

    for k in range(nch):
        pair_copy(k).wait_recv()
        mine[k] = mine[k] + recv_p[k]

    def line_copy(k, right):
        src, dst, ss, rs = (rout, rin, r_s, r_r) if right else (lout, lin, l_s, l_r)
        to = jnp.minimum(z + 1, nz - 1) if right else jnp.maximum(z - 1, 0)
        return pltpu.make_async_remote_copy(
            src_ref=src.at[k], dst_ref=dst.at[k], send_sem=ss.at[k], recv_sem=rs.at[k],
            device_id={"taps": to}, device_id_type=MESH,
        )

    def line_step(s, carry):
        for right in (True, False):
            hop = z if right else nz - 1 - z
            k = s - LAG * hop
            came, out = (rin, rout) if right else (lin, lout)

            @pl.when(jnp.logical_and(k >= 0, k < nch))
            def _():
                @pl.when(hop > 0)
                def _():
                    line_copy(k, right).wait_recv()

                @pl.when(hop < nz - 1)
                def _():
                    out[k] = mine[k] + came[k]
                    line_copy(k, right).start()

        return carry

    lax.fori_loop(0, nch + LAG * (nz - 1), line_step, 0)

    mode_ids = lax.broadcasted_iota(jnp.int32, (md, modes), 1)

    def pick(owner):
        mine_order = order_ref[pl.ds(pl.multiple_of(owner * md, md), md), :]
        return mine_order == mode_ids

    def shapes(hot):
        return dot_nt(hot.astype(f32).astype(bf16), shape_ref[...]).astype(bf16)

    hot_me = pick(me)
    hot_other = pick(z * nc + other)
    g_both = jnp.concatenate([shapes(hot_other), shapes(hot_me)], axis=0)
    d = jnp.sum(jnp.where(hot_me, decay_ref[...], 0.0), axis=1, keepdims=True)
    w = jnp.sum(jnp.where(hot_me, freq_ref[...], 0.0), axis=1, keepdims=True)
    ls = dot_nt(fshape_ref[...], hot_me.astype(f32).astype(bf16)).astype(bf16)
    e2 = 2.0 * d
    series = 1.0 / 40320.0
    poly = jnp.full_like(e2, series)
    for coef in (1.0 / 5040, 1.0 / 720, 1.0 / 120, 1.0 / 24, 1.0 / 6, 0.5, 1.0):
        poly = coef - e2 * poly
    gain = jnp.sqrt(e2 * poly)
    ahead = (lax.broadcasted_iota(jnp.int32, (md, LANES), 1) + 1).astype(f32)
    mag = jnp.exp(-d * ahead)
    t_re = mag * jnp.cos(w * ahead)
    t_im = mag * jnp.sin(w * ahead)
    tabs[0] = t_re
    tabs[1] = t_im
    lane = lax.broadcasted_iota(jnp.int32, (md, LANES), 1)

    floor_row = lax.broadcasted_iota(jnp.int32, (floors, LANES), 0)

    def pick_loads(q, owner, lo):
        for r in range(fd):
            lo.append(jnp.sum(jnp.where(floor_row == owner * fd + r, q, 0.0), axis=0, keepdims=True))

    for tb in range(tblocks):
        parts = []
        for s in range(splits):
            k = tb * splits + s
            parts.append(mine[k] + rin[k] + lin[k])
        q = jnp.concatenate(parts, axis=0)
        both = dot_split(g_both, q[:panels])
        cols = slice(tb * LANES, (tb + 1) * LANES)
        xs[0:md, cols] = both[:md]
        fb[c, 0:md, cols] = both[md:]
        theirs, ours = [], []
        pick_loads(q[panels:], z * nc + other, theirs)
        pick_loads(q[panels:], me, ours)
        for r in range(fd):
            xs[md + r : md + r + 1, cols] = theirs[r]
            fb[c, md + r : md + r + 1, cols] = ours[r]
    pad = xs.shape[0] - md - fd
    if pad:
        xs[md + fd :, :] = jnp.zeros((pad, th), f32)
        fb[c, md + fd :, :] = jnp.zeros((pad, th), f32)
    ex = pltpu.make_async_remote_copy(
        src_ref=xs, dst_ref=fb.at[c], send_sem=x_s, recv_sem=x_r,
        device_id={"floors": other}, device_id_type=MESH,
    )
    ex.start()
    ex.wait_recv()

    end_re, end_im = [], []
    coefs = []
    step = 1
    while step < LANES:
        keep = lane >= step
        coefs.append(
            (
                step,
                jnp.where(keep, t_re[:, step - 1 : step], 0.0),
                jnp.where(keep, t_im[:, step - 1 : step], 0.0),
            )
        )
        step *= 2
    for i, (_, a, b) in enumerate(coefs):
        tabs[2 + 2 * i] = a
        tabs[3 + 2 * i] = b
    nb = time_dev // LANES
    for blk in range(nb):
        h, tb = blk // tblocks, blk % tblocks
        re = gain * fb[h, 0:md, tb * LANES : (tb + 1) * LANES]
        im = None
        for i, (step, _, _) in enumerate(coefs):
            a, b = tabs[2 + 2 * i], tabs[3 + 2 * i]
            rr = pltpu.roll(re, step, 1)
            if im is None:
                re, im = re + a * rr, b * rr
            else:
                ri = pltpu.roll(im, step, 1)
                re, im = re + a * rr - b * ri, im + a * ri + b * rr
        loc[blk] = re
        end_re.append(re[:, LANES - 1 :])
        end_im.append(im[:, LANES - 1 :])

    zb_re, zb_im = t_re[:, LANES - 1 :], t_im[:, LANES - 1 :]
    s_re, s_im = end_re[0], end_im[0]
    for blk in range(1, nb):
        s_re, s_im = (
            zb_re * s_re - zb_im * s_im + end_re[blk],
            zb_im * s_re + zb_re * s_im + end_im[blk],
        )

    def state_copy(to, src):
        return pltpu.make_async_remote_copy(
            src_ref=st_send, dst_ref=st_recv.at[src], send_sem=t_s.at[to], recv_sem=t_r.at[src],
            device_id={"tm": to}, device_id_type=MESH,
        )

    st_send[...] = jnp.where(lane == 0, s_re, s_im)
    in_re = jnp.zeros((md, 1), f32)
    in_im = jnp.zeros((md, 1), f32)
    if ntm > 1:
        for to in range(1, ntm):

            @pl.when(x < to)
            def _():
                state_copy(to, jnp.minimum(x, ntm - 2)).start()

        for src in range(ntm - 1):

            @pl.when(x > src)
            def _():
                state_copy(lax.rem(x + 1, ntm), src).wait_recv()

            @pl.when(x <= src)
            def _():
                st_recv[src] = jnp.zeros_like(st_send)

            length = (jnp.maximum(x - 1 - src, 0) * time_dev).astype(f32)
            pm = jnp.exp(-d * length)
            pr, pi = pm * jnp.cos(w * length), pm * jnp.sin(w * length)
            got_re, got_im = st_recv[src][:, 0:1], st_recv[src][:, 1:2]
            in_re = in_re + pr * got_re - pi * got_im
            in_im = in_im + pi * got_re + pr * got_im

    t_re, t_im = tabs[0], tabs[1]
    for blk in range(nb):
        y = loc[blk] + t_re * in_re - t_im * in_im
        cols = slice(blk * LANES, (blk + 1) * LANES)
        y_ref[:, cols] = y
        in_re, in_im = (
            zb_re * in_re - zb_im * in_im + end_re[blk],
            zb_im * in_re + zb_re * in_im + end_im[blk],
        )
        part = dot_split(ls, y)
        for j in range(owners):
            fs[j, :, cols] = part[j * fd : (j + 1) * fd]

    def motion_copy(k):
        j = lax.rem(me + k, owners)
        return pltpu.make_async_remote_copy(
            src_ref=fs.at[j], dst_ref=fr.at[me], send_sem=f_s.at[k], recv_sem=f_r.at[k],
            device_id={"taps": j // nc, "floors": lax.rem(j, nc)}, device_id_type=MESH,
        )

    def motion_start(k, carry):
        motion_copy(k).start()
        return carry

    def motion_recv(k, total):
        motion_copy(k).wait_recv()
        return total + fr[lax.rem(me + owners - k, owners)]

    def motion_sent(k, carry):
        motion_copy(k).wait_send()
        return carry

    lax.fori_loop(1, owners, motion_start, 0)
    load_scale = (floors / (taps * owners)) ** 0.5
    for h in range(nc):
        fl_ref[:, h * th : (h + 1) * th] = fb[h, md : md + fd, :] * load_scale

    for k in range(nch):
        pair_copy(k).wait_send()

    def line_sent(k, carry):
        @pl.when(z < nz - 1)
        def _():
            line_copy(k, True).wait_send()

        @pl.when(z > 0)
        def _():
            line_copy(k, False).wait_send()

        return carry

    lax.fori_loop(0, nch, line_sent, 0)
    ex.wait_send()
    for to in range(1, ntm):

        @pl.when(x < to)
        def _():
            state_copy(to, jnp.minimum(x, ntm - 2)).wait_send()

    fm_ref[...] = lax.fori_loop(1, owners, motion_recv, fs[me])
    lax.fori_loop(1, owners, motion_sent, 0)


def on_device(
    pressures, tap_area, tap_panel, tap_floor, panel_shape, floor_shape, mode_order, mode_decay, mode_freq
):
    nz, nc, ntm = lax.axis_size("taps"), lax.axis_size("floors"), lax.axis_size("tm")
    owners = nz * nc
    time_dev, taps = pressures.shape
    panels, modes = panel_shape.shape
    floors = floor_shape.shape[0]
    rows = panels + floors
    splits = 2
    th = time_dev // nc
    md, fd = modes // owners, floors // owners
    nch = th // LANES * splits
    xrows = md + -(-fd // 8) * 8
    chunk = pltpu.VMEM((nch, rows // splits, LANES), jnp.float32)
    vmem = pl.BlockSpec(memory_space=pltpu.VMEM)
    dma = pltpu.SemaphoreType.DMA
    f32 = jnp.float32
    out = pl.pallas_call(
        functools.partial(kernel, (nz, nc, ntm, splits)),
        out_shape=(
            jax.ShapeDtypeStruct((md, time_dev), f32),
            jax.ShapeDtypeStruct((fd, time_dev), f32),
            jax.ShapeDtypeStruct((fd, time_dev), f32),
        ),
        in_specs=[pl.BlockSpec(memory_space=pl.ANY)] + [vmem] * 8,
        out_specs=(vmem,) * 3,
        scratch_shapes=[
            pltpu.VMEM((time_dev, taps), jnp.bfloat16),
            pltpu.VMEM((rows, taps), jnp.bfloat16),
            chunk, chunk, chunk, chunk, chunk, chunk, chunk,
            pltpu.VMEM((xrows, th), f32),
            pltpu.VMEM((nc, xrows, th), f32),
            pltpu.VMEM((16, md, LANES), f32),
            pltpu.VMEM((time_dev // LANES, md, LANES), f32),
            pltpu.VMEM((md, LANES), f32),
            pltpu.VMEM((max(ntm - 1, 1), md, LANES), f32),
            pltpu.VMEM((owners, fd, time_dev), f32),
            pltpu.VMEM((owners, fd, time_dev), f32),
            dma((2 * (th // min(256, th)),)),
            dma((nch,)), dma((nch,)), dma((nch,)), dma((nch,)), dma((nch,)), dma((nch,)),
            dma, dma,
            dma((ntm,)), dma((ntm,)),
            dma((owners,)), dma((owners,)),
        ],
        compiler_params=pltpu.CompilerParams(
            collective_id=0, has_side_effects=True, vmem_limit_bytes=48 * 1024 * 1024
        ),
    )(
        pressures,
        tap_area.reshape(1, taps),
        tap_panel.reshape(1, taps),
        tap_floor.reshape(1, taps),
        panel_shape,
        floor_shape,
        mode_order.reshape(modes, 1),
        mode_decay.reshape(1, modes),
        mode_freq.reshape(1, modes),
    )
    return out


def solution(mesh):
    own = P(("taps", "floors"))
    out_spec = P(("taps", "floors"), ("dirs", "tm"))
    return jax.shard_map(
        on_device,
        mesh=mesh,
        in_specs=(P(("dirs", "tm"), ("taps", "floors")), own, own, own, P(), P(), P(), P(), P()),
        out_specs=(out_spec, out_spec, out_spec),
        check_vma=False,
    )
```

time: 211 us -> 49.9 us (0.24); the launches traced: 207 us -> 49.1 us
  matrix products: 83.3 us -> 0 us
  waiting for transfers between devices: 79.7 us -> 0 us
  Pallas kernels: 0 us -> 38.4 us
  between operations: 15.6 us -> 0.66 us
  local copies, waits for them, and re-layouts: 18 us -> 10 us
  other arithmetic: 6.88 us -> 0 us
  blocking collectives: 3.76 us -> 0 us
    dot_general x6 -> x0, matrix products: 83.3 us -> none  [the longest x1 70.5 us: on_device(): jnp.einsum('mij,mbj->mbi', toeplitz, force_blocks, precision=highest)]
    unnamed x3 -> x0, waiting for transfers between devices: 54.7 us -> none
    pallas_call x0 -> x1, Pallas kernels: none -> 38.4 us  [on_device(): pl.pallas_call(functools.partial(kernel, (nz, nc, ntm, splits)), out_shap...]
    reduce_scatter x1 -> x0, waiting for transfers between devices: 25 us -> none  [on_device(): lax.psum_scatter(lax.dot_general(tributary, pressures, (((0,), (1,)), (()...]
    gather x5 -> x0, local copies, waits for them, and re-layouts: 11.7 us -> none  [the longest x1 7.54 us: on_device(): jnp.take(ordered, tap_panel, axis=0).astype(jnp.float32)]
    unnamed x26 -> x17, local copies, waits for them, and re-layouts: 4.29 us -> 8.51 us
    unnamed x1 -> x0, blocking collectives: 3.76 us -> none
    and x3 -> x0, other arithmetic: 2.15 us -> none  [the longest x1 0.76 us: on_device(): decays = jnp.take(mode_decay, local_order)]
  transfers between devices with their start and end apart: 2 -> 0, of which waited for: 2 -> 0; matrix products, arithmetic and copies ran while one was open for 4% -> 0% of each run, Pallas kernels for 0% -> 0%
where the time goes in v1:
time: 49.9 us; the launch traced here: 49.1 us
  Pallas kernels  38.4 us (77%)
  local copies, waits for them, and re-layouts  10 us (20%)
  between operations  0.66 us (1%)
    pallas_call x1, Pallas kernels, on_device(): pl.pallas_call(functools.partial(kernel, (nz, nc, ntm, splits)), out_shap...  38.4 us
    unnamed x17, local copies, waits for them, and re-layouts  8.51 us

profile of v1, /device:TPU:3, one launch (start us, length us, event | category | flops | bytes accessed | tf_op | source)
XLA Modules:
  0.0 49.1 jit_solution(5073729225140513573)
XLA Ops:
  0.6 0.7 %reshape.24.area_ref = bf16[1,2048]{1,0:T(2,128)(2,1)S(1)} reshape(bf16[2048]{0:T(1024)(128)(2,1)} %param.10) | data formatting | bytes 8192 | tf_op jit(solution)/shard_map/reshape | solution.py:406
  1.3 0.8 %copy.12.order_ref = s32[512,1]{1,0:T(8,128)S(1)} copy(s32[512,1]{0,1:T(1,128)} %bitcast.9) | data formatting | bytes 4096 | tf_op jit(solution)/shard_map/reshape | solution.py:411
  2.2 0.0 copy-start
  2.2 2.2 %copy-done = bf16[1024,2048]{1,0:T(8,128)(2,1)S(1)} copy-done((bf16[1024,2048]{1,0:T(8,128)(2,1)S(1)}, bf16[1024,2048]{1,0:T(8,128)(2,1)}, u32[]{:S(2)}) %copy-start) | copy-done | bytes 4194328
  4.3 0.0 copy-start.1
  4.3 0.9 %copy-done.1 = bf16[256,512]{1,0:T(8,128)(2,1)S(1)} copy-done((bf16[256,512]{1,0:T(8,128)(2,1)S(1)}, bf16[256,512]{1,0:T(8,128)(2,1)}, u32[]{:S(2)}) %copy-start.1) | copy-done | bytes 262168
  5.3 0.0 copy-start.2
  5.3 0.7 %copy-done.2 = bf16[16,512]{1,0:T(8,128)(2,1)S(1)} copy-done((bf16[16,512]{1,0:T(8,128)(2,1)S(1)}, bf16[16,512]{1,0:T(8,128)(2,1)}, u32[]{:S(2)}) %copy-start.2) | copy-done | bytes 16408
  6.0 0.0 copy-start.3
  6.0 0.7 %copy-done.3 = s32[2048]{0:T(1024)S(1)} copy-done((s32[2048]{0:T(1024)S(1)}, s32[2048]{0:T(1024)}, u32[]{:S(2)}) %copy-start.3) | copy-done | bytes 8216
  6.7 0.0 copy-start.4
  6.7 0.7 %copy-done.4 = s32[2048]{0:T(1024)S(1)} copy-done((s32[2048]{0:T(1024)S(1)}, s32[2048]{0:T(1024)}, u32[]{:S(2)}) %copy-start.4) | copy-done | bytes 8216
  7.4 0.0 copy-start.5
  7.4 0.7 %copy-done.5 = f32[512]{0:T(512)S(1)} copy-done((f32[512]{0:T(512)S(1)}, f32[512]{0:T(512)}, u32[]{:S(2)}) %copy-start.5) | copy-done | bytes 2072
  8.1 0.0 copy-start.6
  8.1 0.7 %copy-done.6 = f32[512]{0:T(512)S(1)} copy-done((f32[512]{0:T(512)S(1)}, f32[512]{0:T(512)}, u32[]{:S(2)}) %copy-start.6) | copy-done | bytes 2072
  8.8 38.4 %shard_map.112 = (f32[64,1024]{1,0:T(8,128)S(1)}, f32[2,1024]{1,0:T(2,128)S(1)}, f32[2,1024]{1,0:T(2,128)S(1)}) custom-call(bf16[1024,2048]{1,0:T(8,128)(2,1)S(1)} %copy-done, bf16[1,2048]{1,0:T(2,128)(2,1)S(1)} %reshape.24.area_ref, s32[1,2048]{1,0:T(1,128)S(1)} %bitcast.5, s32[1,2048]{1,0:T(1,128)S(1)} %bitcast.6, bf16[256,512]{1,0:T(8,128)(2,1)S(1)} %copy-done.1, ...), custom_call_target="tpu_custom_call" | custom-call | tf_op jit(solution)/shard_map/pallas_call | solution.py:374
  47.2 0.7 %copy.16 = f32[64,1024]{1,0:T(8,128)} copy(f32[64,1024]{1,0:T(8,128)S(1)} %get-tuple-element.6) | data formatting | bytes 524288
  47.9 0.6 %copy.17 = f32[2,1024]{1,0:T(2,128)} copy(f32[2,1024]{1,0:T(2,128)S(1)} %get-tuple-element.7) | data formatting | bytes 16384
  48.5 0.6 %copy.18 = f32[2,1024]{1,0:T(2,128)} copy(f32[2,1024]{1,0:T(2,128)S(1)} %get-tuple-element.8) | data formatting | bytes 16384
Async XLA Ops:
  2.2 2.2 %copy-start = (bf16[1024,2048]{1,0:T(8,128)(2,1)S(1)}, bf16[1024,2048]{1,0:T(8,128)(2,1)}, u32[]{:S(2)}) copy-start(bf16[1024,2048]{1,0:T(8,128)(2,1)} %p_hbm.1) | copy-start | bytes 12582916
  4.3 0.9 %copy-start.1 = (bf16[256,512]{1,0:T(8,128)(2,1)S(1)}, bf16[256,512]{1,0:T(8,128)(2,1)}, u32[]{:S(2)}) copy-start(bf16[256,512]{1,0:T(8,128)(2,1)} %shape_ref.1) | copy-start | bytes 786436
  5.3 0.7 %copy-start.2 = (bf16[16,512]{1,0:T(8,128)(2,1)S(1)}, bf16[16,512]{1,0:T(8,128)(2,1)}, u32[]{:S(2)}) copy-start(bf16[16,512]{1,0:T(8,128)(2,1)} %fshape_ref.1) | copy-start | bytes 49156
  6.0 0.7 %copy-start.3 = (s32[2048]{0:T(1024)S(1)}, s32[2048]{0:T(1024)}, u32[]{:S(2)}) copy-start(s32[2048]{0:T(1024)} %param.11) | copy-start | bytes 24580
  6.7 0.7 %copy-start.4 = (s32[2048]{0:T(1024)S(1)}, s32[2048]{0:T(1024)}, u32[]{:S(2)}) copy-start(s32[2048]{0:T(1024)} %param.12) | copy-start | bytes 24580
  7.4 0.7 %copy-start.5 = (f32[512]{0:T(512)S(1)}, f32[512]{0:T(512)}, u32[]{:S(2)}) copy-start(f32[512]{0:T(512)} %param.16) | copy-start | bytes 6148
  8.1 0.7 %copy-start.6 = (f32[512]{0:T(512)S(1)}, f32[512]{0:T(512)}, u32[]{:S(2)}) copy-start(f32[512]{0:T(512)} %param.17) | copy-start | bytes 6148

commit v2 on v1

--- a/solution.py
+++ b/solution.py
@@ -27,11 +27,12 @@
 
 def kernel(
     cfg,
-    p_hbm, area_ref, panel_ref, floor_ref, shape_ref, fshape_ref, order_ref, decay_ref, freq_ref,
+    p_hbm, area_h, panel_h, floor_h, shape_h, fshape_h, order_h, decay_h, freq_h,
     y_ref, fm_ref, fl_ref,
-    pv, w_ref, mine, send_p, recv_p, rin, lin, rout, lout, xs, fb, tabs, loc, st_send, st_recv,
+    area_ref, panel_ref, floor_ref, shape_ref, fshape_ref, order_ref, decay_ref, freq_ref, order_col,
+    pv, w_ref, mine, send_p, recv_p, rin, lin, rout, lout, xs, fb, tabs, loc, loc_im, st_send, st_recv,
     fs, fr,
-    p_sem, pp_s, pp_r, r_s, r_r, l_s, l_r, x_s, x_r, t_s, t_r, f_s, f_r,
+    in_sem, p_sem, pp_s, pp_r, r_s, r_r, l_s, l_r, x_s, x_r, t_s, t_r, f_s, f_r,
 ):
     nz, nc, ntm, splits = cfg
     owners = nz * nc
@@ -53,6 +54,18 @@
     f32 = jnp.float32
     bf16 = jnp.bfloat16
 
+    small = [
+        pltpu.make_async_copy(src, dst, in_sem.at[i])
+        for i, (src, dst) in enumerate(
+            (
+                (area_h, area_ref), (panel_h, panel_ref), (floor_h, floor_ref), (shape_h, shape_ref),
+                (fshape_h, fshape_ref), (order_h, order_ref), (decay_h, decay_ref), (freq_h, freq_ref),
+            )
+        )
+    ]
+    for cp in small:
+        cp.start()
+
     barrier = pltpu.get_barrier_semaphore()
 
     def greet(k, carry):
@@ -81,11 +94,16 @@
             cp.start()
             loads.append((cp, off))
 
+    for cp in small[:3]:
+        cp.wait()
+    ids = lax.broadcasted_iota(jnp.int32, (panels, LANES), 0)
+    fids = lax.broadcasted_iota(jnp.int32, (floors, LANES), 0)
     area = area_ref[...].astype(f32)
-    ids = lax.broadcasted_iota(jnp.int32, (panels, taps), 0)
-    w_ref[0:panels, :] = jnp.where(panel_ref[...] == ids, area, 0.0).astype(bf16)
-    fids = lax.broadcasted_iota(jnp.int32, (floors, taps), 0)
-    w_ref[panels:rows, :] = jnp.where(floor_ref[...] == fids, area, 0.0).astype(bf16)
+    for r in range(taps // LANES):
+        cols = slice(r * LANES, (r + 1) * LANES)
+        row = area[r : r + 1, :]
+        w_ref[0:panels, cols] = jnp.where(panel_ref[:, cols] == ids, row, 0.0).astype(bf16)
+        w_ref[panels:rows, cols] = jnp.where(floor_ref[:, cols] == fids, row, 0.0).astype(bf16)
 
     def sums(b, h, dst):
         cp, off = loads[h * per_half + b]
@@ -104,61 +122,70 @@
         )
 
     per_step = step_t // LANES * splits
+
+    @pl.when(z == 0)
+    def _():
+        rin[...] = jnp.zeros_like(rin)
+
+    @pl.when(z == nz - 1)
+    def _():
+        lin[...] = jnp.zeros_like(lin)
+
+    def line_copy(k, right):
+        src, dst, ss, rs = (rout, rin, r_s, r_r) if right else (lout, lin, l_s, l_r)
+        to = jnp.minimum(z + 1, nz - 1) if right else jnp.maximum(z - 1, 0)
+        return pltpu.make_async_remote_copy(
+            src_ref=src.at[k], dst_ref=dst.at[k], send_sem=ss.at[k], recv_sem=rs.at[k],
+            device_id={"taps": to}, device_id_type=MESH,
+        )
+
+    def line_step(s, carry):
+        for right in (True, False):
+            hop = z if right else nz - 1 - z
+            k = s - LAG * hop
+            came, out = (rin, rout) if right else (lin, lout)
+
+            @pl.when(jnp.logical_and(k >= 0, k < nch))
+            def _():
+                @pl.when(hop > 0)
+                def _():
+                    line_copy(k, right).wait_recv()
+
+                @pl.when(hop < nz - 1)
+                def _():
+                    out[k] = mine[k] + came[k]
+                    line_copy(k, right).start()
+
+        return carry
+
+    def merge(b):
+        for k in range(b * per_step, (b + 1) * per_step):
+            pair_copy(k).wait_recv()
+            mine[k] = mine[k] + recv_p[k]
+
     for b in range(per_half):
         sums(b, 0, send_p)
         if b == 0:
             pl.semaphore_wait(barrier, owners - 1 + ntm - 1)
         for k in range(b * per_step, (b + 1) * per_step):
             pair_copy(k).start()
-    for b in range(per_half):
         sums(b, 1, mine)
-
-    @pl.when(z == 0)
-    def _():
-        rin[...] = jnp.zeros_like(rin)
-
-    @pl.when(z == nz - 1)
-    def _():
-        lin[...] = jnp.zeros_like(lin)
-
-    for k in range(nch):
-        pair_copy(k).wait_recv()
-        mine[k] = mine[k] + recv_p[k]
-
-    def line_copy(k, right):
-        src, dst, ss, rs = (rout, rin, r_s, r_r) if right else (lout, lin, l_s, l_r)
-        to = jnp.minimum(z + 1, nz - 1) if right else jnp.maximum(z - 1, 0)
-        return pltpu.make_async_remote_copy(
-            src_ref=src.at[k], dst_ref=dst.at[k], send_sem=ss.at[k], recv_sem=rs.at[k],
-            device_id={"taps": to}, device_id_type=MESH,
-        )
-
-    def line_step(s, carry):
-        for right in (True, False):
-            hop = z if right else nz - 1 - z
-            k = s - LAG * hop
-            came, out = (rin, rout) if right else (lin, lout)
-
-            @pl.when(jnp.logical_and(k >= 0, k < nch))
-            def _():
-                @pl.when(hop > 0)
-                def _():
-                    line_copy(k, right).wait_recv()
-
-                @pl.when(hop < nz - 1)
-                def _():
-                    out[k] = mine[k] + came[k]
-                    line_copy(k, right).start()
-
-        return carry
-
-    lax.fori_loop(0, nch + LAG * (nz - 1), line_step, 0)
-
-    mode_ids = lax.broadcasted_iota(jnp.int32, (md, modes), 1)
+        if b > 0:
+            merge(b - 1)
+        if b == 1:
+            lax.fori_loop(0, min(LAG, per_step), line_step, 0)
+    merge(per_half - 1)
+    first = min(LAG, per_step) if per_half > 1 else 0
+    early = min(LAG + 2, nch)
+    lax.fori_loop(first, early, line_step, 0)
+
+    for cp in small[3:]:
+        cp.wait()
+    order_col[...] = jnp.transpose(jnp.broadcast_to(order_ref[...].astype(f32), (LANES, modes)))
+    mode_ids = lax.broadcasted_iota(jnp.int32, (md, modes), 1).astype(f32)
 
     def pick(owner):
-        mine_order = order_ref[pl.ds(pl.multiple_of(owner * md, md), md), :]
-        return mine_order == mode_ids
+        return order_col[pl.ds(pl.multiple_of(owner * md, md), md), 0:1] == mode_ids
 
     def shapes(hot):
         return dot_nt(hot.astype(f32).astype(bf16), shape_ref[...]).astype(bf16)
@@ -170,74 +197,55 @@
     w = jnp.sum(jnp.where(hot_me, freq_ref[...], 0.0), axis=1, keepdims=True)
     ls = dot_nt(fshape_ref[...], hot_me.astype(f32).astype(bf16)).astype(bf16)
     e2 = 2.0 * d
-    series = 1.0 / 40320.0
-    poly = jnp.full_like(e2, series)
+    poly = jnp.full_like(e2, 1.0 / 40320.0)
     for coef in (1.0 / 5040, 1.0 / 720, 1.0 / 120, 1.0 / 24, 1.0 / 6, 0.5, 1.0):
         poly = coef - e2 * poly
     gain = jnp.sqrt(e2 * poly)
-    ahead = (lax.broadcasted_iota(jnp.int32, (md, LANES), 1) + 1).astype(f32)
+    lane = lax.broadcasted_iota(jnp.int32, (md, LANES), 1)
+    ahead = (lane + 1).astype(f32)
     mag = jnp.exp(-d * ahead)
     t_re = mag * jnp.cos(w * ahead)
     t_im = mag * jnp.sin(w * ahead)
     tabs[0] = t_re
     tabs[1] = t_im
-    lane = lax.broadcasted_iota(jnp.int32, (md, LANES), 1)
-
-    floor_row = lax.broadcasted_iota(jnp.int32, (floors, LANES), 0)
-
-    def pick_loads(q, owner, lo):
-        for r in range(fd):
-            lo.append(jnp.sum(jnp.where(floor_row == owner * fd + r, q, 0.0), axis=0, keepdims=True))
-
-    for tb in range(tblocks):
-        parts = []
-        for s in range(splits):
-            k = tb * splits + s
-            parts.append(mine[k] + rin[k] + lin[k])
-        q = jnp.concatenate(parts, axis=0)
-        both = dot_split(g_both, q[:panels])
-        cols = slice(tb * LANES, (tb + 1) * LANES)
-        xs[0:md, cols] = both[:md]
-        fb[c, 0:md, cols] = both[md:]
-        theirs, ours = [], []
-        pick_loads(q[panels:], z * nc + other, theirs)
-        pick_loads(q[panels:], me, ours)
-        for r in range(fd):
-            xs[md + r : md + r + 1, cols] = theirs[r]
-            fb[c, md + r : md + r + 1, cols] = ours[r]
-    pad = xs.shape[0] - md - fd
-    if pad:
-        xs[md + fd :, :] = jnp.zeros((pad, th), f32)
-        fb[c, md + fd :, :] = jnp.zeros((pad, th), f32)
-    ex = pltpu.make_async_remote_copy(
-        src_ref=xs, dst_ref=fb.at[c], send_sem=x_s, recv_sem=x_r,
-        device_id={"floors": other}, device_id_type=MESH,
-    )
-    ex.start()
-    ex.wait_recv()
-
-    end_re, end_im = [], []
-    coefs = []
+    hops = []
     step = 1
     while step < LANES:
-        keep = lane >= step
-        coefs.append(
-            (
-                step,
-                jnp.where(keep, t_re[:, step - 1 : step], 0.0),
-                jnp.where(keep, t_im[:, step - 1 : step], 0.0),
-            )
-        )
+        i = 2 + 2 * len(hops)
+        tabs[i] = jnp.where(lane >= step, t_re[:, step - 1 : step], 0.0)
+        tabs[i + 1] = jnp.where(lane >= step, t_im[:, step - 1 : step], 0.0)
+        hops.append(step)
         step *= 2
-    for i, (_, a, b) in enumerate(coefs):
-        tabs[2 + 2 * i] = a
-        tabs[3 + 2 * i] = b
-    nb = time_dev // LANES
-    for blk in range(nb):
-        h, tb = blk // tblocks, blk % tblocks
-        re = gain * fb[h, 0:md, tb * LANES : (tb + 1) * LANES]
+
+    floor_row = lax.broadcasted_iota(jnp.int32, (floors, LANES), 0)
+
+    def load_row(q, row):
+        return jnp.sum(jnp.where(floor_row == row, q, 0.0), axis=0, keepdims=True)
+
+    def exchange(tb):
+        return pltpu.make_async_remote_copy(
+            src_ref=xs.at[tb], dst_ref=fb.at[c * tblocks + tb],
+            send_sem=x_s.at[tb], recv_sem=x_r.at[tb],
+            device_id={"floors": other}, device_id_type=MESH,
+        )
+
+    def forces(tb):
+        q = jnp.concatenate(
+            [mine[k] + rin[k] + lin[k] for k in range(tb * splits, (tb + 1) * splits)], axis=0
+        )
+        both = dot_split(g_both, q[:panels])
+        blk = c * tblocks + tb
+        pad = [jnp.zeros((xs.shape[1] - md - fd, LANES), f32)] if xs.shape[1] > md + fd else []
+        theirs = [load_row(q[panels:], (z * nc + other) * fd + r) for r in range(fd)]
+        ours = [load_row(q[panels:], me * fd + r) for r in range(fd)]
+        xs[tb] = jnp.concatenate([both[:md]] + theirs + pad, axis=0)
+        exchange(tb).start()
+        fb[blk] = jnp.concatenate([both[md:]] + ours + pad, axis=0)
+
+    def at_rest(blk):
+        re = gain * fb[blk, 0:md, :]
         im = None
-        for i, (step, _, _) in enumerate(coefs):
+        for i, step in enumerate(hops):
             a, b = tabs[2 + 2 * i], tabs[3 + 2 * i]
             rr = pltpu.roll(re, step, 1)
             if im is None:
@@ -246,8 +254,23 @@
                 ri = pltpu.roll(im, step, 1)
                 re, im = re + a * rr - b * ri, im + a * ri + b * rr
         loc[blk] = re
-        end_re.append(re[:, LANES - 1 :])
-        end_im.append(im[:, LANES - 1 :])
+        loc_im[blk] = im
+
+    done = early
+    for tb in range(tblocks):
+        upto = (tb + 1) * splits + LAG * (nz - 1)
+        lax.fori_loop(done, upto, line_step, 0)
+        done = upto
+        forces(tb)
+        at_rest(c * tblocks + tb)
+        if tb > 0:
+            exchange(tb - 1).wait_recv()
+            at_rest(other * tblocks + tb - 1)
+    exchange(tblocks - 1).wait_recv()
+    at_rest(other * tblocks + tblocks - 1)
+    nb = time_dev // LANES
+    end_re = [loc[blk][:, LANES - 1 :] for blk in range(nb)]
+    end_im = [loc_im[blk][:, LANES - 1 :] for blk in range(nb)]
 
     zb_re, zb_im = t_re[:, LANES - 1 :], t_im[:, LANES - 1 :]
     s_re, s_im = end_re[0], end_im[0]
@@ -324,8 +347,8 @@
 
     lax.fori_loop(1, owners, motion_start, 0)
     load_scale = (floors / (taps * owners)) ** 0.5
-    for h in range(nc):
-        fl_ref[:, h * th : (h + 1) * th] = fb[h, md : md + fd, :] * load_scale
+    for blk in range(nb):
+        fl_ref[:, blk * LANES : (blk + 1) * LANES] = fb[blk, md : md + fd, :] * load_scale
 
     for k in range(nch):
         pair_copy(k).wait_send()
@@ -342,7 +365,8 @@
         return carry
 
     lax.fori_loop(0, nch, line_sent, 0)
-    ex.wait_send()
+    for tb in range(tblocks):
+        exchange(tb).wait_send()
     for to in range(1, ntm):
 
         @pl.when(x < to)
@@ -351,6 +375,17 @@
 
     fm_ref[...] = lax.fori_loop(1, owners, motion_recv, fs[me])
     lax.fori_loop(1, owners, motion_sent, 0)
+
+
+def write_out(y, fm, fl, y_out, fm_out, fl_out, sem):
+    copies = [
+        pltpu.make_async_copy(src, dst, sem.at[i])
+        for i, (src, dst) in enumerate(((y, y_out), (fm, fm_out), (fl, fl_out)))
+    ]
+    for cp in copies:
+        cp.start()
+    for cp in copies:
+        cp.wait()
 
 
 def on_device(
@@ -378,41 +413,59 @@
             jax.ShapeDtypeStruct((fd, time_dev), f32),
             jax.ShapeDtypeStruct((fd, time_dev), f32),
         ),
-        in_specs=[pl.BlockSpec(memory_space=pl.ANY)] + [vmem] * 8,
+        in_specs=[pl.BlockSpec(memory_space=pltpu.HBM)] * 9,
         out_specs=(vmem,) * 3,
         scratch_shapes=[
+            pltpu.VMEM((taps // LANES, LANES), jnp.bfloat16),
+            pltpu.VMEM((1, taps), jnp.int32),
+            pltpu.VMEM((1, taps), jnp.int32),
+            pltpu.VMEM(panel_shape.shape, jnp.bfloat16),
+            pltpu.VMEM(floor_shape.shape, jnp.bfloat16),
+            pltpu.VMEM((1, modes), jnp.int32),
+            pltpu.VMEM((1, modes), f32),
+            pltpu.VMEM((1, modes), f32),
+            pltpu.VMEM((modes, LANES), f32),
             pltpu.VMEM((time_dev, taps), jnp.bfloat16),
             pltpu.VMEM((rows, taps), jnp.bfloat16),
             chunk, chunk, chunk, chunk, chunk, chunk, chunk,
-            pltpu.VMEM((xrows, th), f32),
-            pltpu.VMEM((nc, xrows, th), f32),
+            pltpu.VMEM((th // LANES, xrows, LANES), f32),
+            pltpu.VMEM((time_dev // LANES, xrows, LANES), f32),
             pltpu.VMEM((16, md, LANES), f32),
+            pltpu.VMEM((time_dev // LANES, md, LANES), f32),
             pltpu.VMEM((time_dev // LANES, md, LANES), f32),
             pltpu.VMEM((md, LANES), f32),
             pltpu.VMEM((max(ntm - 1, 1), md, LANES), f32),
             pltpu.VMEM((owners, fd, time_dev), f32),
             pltpu.VMEM((owners, fd, time_dev), f32),
+            dma((8,)),
             dma((2 * (th // min(256, th)),)),
             dma((nch,)), dma((nch,)), dma((nch,)), dma((nch,)), dma((nch,)), dma((nch,)),
-            dma, dma,
+            dma((th // LANES,)), dma((th // LANES,)),
             dma((ntm,)), dma((ntm,)),
             dma((owners,)), dma((owners,)),
         ],
         compiler_params=pltpu.CompilerParams(
-            collective_id=0, has_side_effects=True, vmem_limit_bytes=48 * 1024 * 1024
+            collective_id=0, has_side_effects=True, vmem_limit_bytes=67043328
         ),
     )(
         pressures,
-        tap_area.reshape(1, taps),
+        tap_area.reshape(taps // LANES, LANES),
         tap_panel.reshape(1, taps),
         tap_floor.reshape(1, taps),
         panel_shape,
         floor_shape,
-        mode_order.reshape(modes, 1),
+        mode_order.reshape(1, modes),
         mode_decay.reshape(1, modes),
         mode_freq.reshape(1, modes),
     )
-    return out
+    return pl.pallas_call(
+        write_out,
+        out_shape=tuple(jax.ShapeDtypeStruct(o.shape, o.dtype) for o in out),
+        in_specs=[vmem] * 3,
+        out_specs=(pl.BlockSpec(memory_space=pltpu.HBM),) * 3,
+        scratch_shapes=[dma((3,))],
+        compiler_params=pltpu.CompilerParams(vmem_limit_bytes=67043328),
+    )(*out)
 
 
 def solution(mesh):

time: 49.9 us -> 40.2 us (0.81); the launches traced: 49.1 us -> 40 us
  local copies, waits for them, and re-layouts: 10 us -> 0 us
  Pallas kernels: 38.4 us -> 39.4 us
    unnamed x17 -> x0, local copies, waits for them, and re-layouts: 8.51 us -> none
    pallas_call x0 -> x1, Pallas kernels: none -> 1.7 us  [on_device(): pl.pallas_call(write_out, out_shape=tuple((jax.ShapeDtypeStruct(o.shape,...]
    reshape x2 -> x0, local copies, waits for them, and re-layouts: 1.51 us -> none  [the longest x1 0.82 us: on_device(): mode_order.reshape(modes, 1)]
    pallas_call x1, Pallas kernels: 38.4 us -> 37.7 us  [on_device(): pl.pallas_call(functools.partial(kernel, (nz, nc, ntm, splits)), out_shap...]
where the time goes in v2:
time: 40.2 us; the launch traced here: 40 us
  Pallas kernels  39.4 us (98%)
  between operations  0.64 us (2%)
    pallas_call x1, Pallas kernels, on_device(): pl.pallas_call(functools.partial(kernel, (nz, nc, ntm, splits)), out_shap...  37.7 us
    pallas_call x1, Pallas kernels, on_device(): pl.pallas_call(write_out, out_shape=tuple((jax.ShapeDtypeStruct(o.shape,...  1.7 us

profile of v2, /device:TPU:3, one launch (start us, length us, event | category | flops | bytes accessed | tf_op | source)
XLA Modules:
  0.0 40.0 jit_solution(17123250667745599047)
XLA Ops:
  0.6 37.7 %shard_map.112 = (f32[64,1024]{1,0:T(8,128)}, f32[2,1024]{1,0:T(2,128)}, f32[2,1024]{1,0:T(2,128)}) custom-call(bf16[1024,2048]{1,0:T(8,128)(2,1)} %p_hbm.1, bf16[16,128]{1,0:T(8,128)(2,1)} %bitcast.8, s32[1,2048]{1,0:T(1,128)} %bitcast.6, s32[1,2048]{1,0:T(1,128)} %bitcast.7, bf16[256,512]{1,0:T(8,128)(2,1)} %shape_h.1, bf16[16,512]{1,0:T(8,128)(2,1)} %fshape_h.1, ...), custom_call_target="tpu_custom_call" | custom-call | tf_op jit(solution)/shard_map/pallas_call | solution.py:409
  38.3 1.7 %shard_map.113 = (f32[64,1024]{1,0:T(8,128)}, f32[2,1024]{1,0:T(2,128)}, f32[2,1024]{1,0:T(2,128)}) custom-call(f32[64,1024]{1,0:T(8,128)} %get-tuple-element.6.y, f32[2,1024]{1,0:T(2,128)} %get-tuple-element.7.fm, f32[2,1024]{1,0:T(2,128)} %get-tuple-element.8.fl), custom_call_target="tpu_custom_call" | custom-call | tf_op jit(solution)/shard_map/pallas_call | solution.py:461

commit v3 on v2

--- a/solution.py
+++ b/solution.py
@@ -169,14 +169,14 @@
             pl.semaphore_wait(barrier, owners - 1 + ntm - 1)
         for k in range(b * per_step, (b + 1) * per_step):
             pair_copy(k).start()
-        sums(b, 1, mine)
         if b > 0:
             merge(b - 1)
         if b == 1:
             lax.fori_loop(0, min(LAG, per_step), line_step, 0)
+        sums(b, 1, mine)
     merge(per_half - 1)
     first = min(LAG, per_step) if per_half > 1 else 0
-    early = min(LAG + 2, nch)
+    early = min(LAG, nch)
     lax.fori_loop(first, early, line_step, 0)
 
     for cp in small[3:]:
@@ -306,10 +306,13 @@
             def _():
                 st_recv[src] = jnp.zeros_like(st_send)
 
+            got_re, got_im = st_recv[src][:, 0:1], st_recv[src][:, 1:2]
+            if ntm == 2:
+                in_re, in_im = got_re, got_im
+                continue
             length = (jnp.maximum(x - 1 - src, 0) * time_dev).astype(f32)
             pm = jnp.exp(-d * length)
             pr, pi = pm * jnp.cos(w * length), pm * jnp.sin(w * length)
-            got_re, got_im = st_recv[src][:, 0:1], st_recv[src][:, 1:2]
             in_re = in_re + pr * got_re - pi * got_im
             in_im = in_im + pi * got_re + pr * got_im
 
@@ -322,9 +325,9 @@
             zb_re * in_re - zb_im * in_im + end_re[blk],
             zb_im * in_re + zb_re * in_im + end_im[blk],
         )
-        part = dot_split(ls, y)
-        for j in range(owners):
-            fs[j, :, cols] = part[j * fd : (j + 1) * fd]
+    part = dot_split(ls, y_ref[...])
+    for j in range(owners):
+        fs[j] = part[j * fd : (j + 1) * fd]
 
     def motion_copy(k):
         j = lax.rem(me + k, owners)

time: 40.2 us -> 39.3 us (0.978)
  Pallas kernels: 39.4 us -> 38.4 us
    pallas_call x1, Pallas kernels: 37.7 us -> 36.7 us  [on_device(): pl.pallas_call(functools.partial(kernel, (nz, nc, ntm, splits)), out_shap...]
where the time goes in v3:
time: 39.3 us; the launch traced here: 39.1 us
  Pallas kernels  38.4 us (98%)
  between operations  0.64 us (2%)
    pallas_call x1, Pallas kernels, on_device(): pl.pallas_call(functools.partial(kernel, (nz, nc, ntm, splits)), out_shap...  36.7 us
    pallas_call x1, Pallas kernels, on_device(): pl.pallas_call(write_out, out_shape=tuple((jax.ShapeDtypeStruct(o.shape,...  1.7 us

profile of v3, /device:TPU:3, one launch (start us, length us, event | category | flops | bytes accessed | tf_op | source)
XLA Modules:
  0.0 39.1 jit_solution(15028898000378080421)
XLA Ops:
  0.6 36.7 %shard_map.112 = (f32[64,1024]{1,0:T(8,128)}, f32[2,1024]{1,0:T(2,128)}, f32[2,1024]{1,0:T(2,128)}) custom-call(bf16[1024,2048]{1,0:T(8,128)(2,1)} %p_hbm.1, bf16[16,128]{1,0:T(8,128)(2,1)} %bitcast.8, s32[1,2048]{1,0:T(1,128)} %bitcast.6, s32[1,2048]{1,0:T(1,128)} %bitcast.7, bf16[256,512]{1,0:T(8,128)(2,1)} %shape_h.1, bf16[16,512]{1,0:T(8,128)(2,1)} %fshape_h.1, ...), custom_call_target="tpu_custom_call" | custom-call | tf_op jit(solution)/shard_map/pallas_call | solution.py:412
  37.4 1.7 %shard_map.113 = (f32[64,1024]{1,0:T(8,128)}, f32[2,1024]{1,0:T(2,128)}, f32[2,1024]{1,0:T(2,128)}) custom-call(f32[64,1024]{1,0:T(8,128)} %get-tuple-element.6.y, f32[2,1024]{1,0:T(2,128)} %get-tuple-element.7.fm, f32[2,1024]{1,0:T(2,128)} %get-tuple-element.8.fl), custom_call_target="tpu_custom_call" | custom-call | tf_op jit(solution)/shard_map/pallas_call | solution.py:464

commit v4 on v3

--- a/solution.py
+++ b/solution.py
@@ -258,7 +258,7 @@
 
     done = early
     for tb in range(tblocks):
-        upto = (tb + 1) * splits + LAG * (nz - 1)
+        upto = max((tb + 1) * splits + LAG * (nz - 1), nch + LAG * (nz - 2))
         lax.fori_loop(done, upto, line_step, 0)
         done = upto
         forces(tb)

time: 39.3 us -> 39.8 us (1.013)
  Pallas kernels: 38.4 us -> 38.9 us
    pallas_call x1, Pallas kernels: 36.7 us -> 37.2 us  [on_device(): pl.pallas_call(functools.partial(kernel, (nz, nc, ntm, splits)), out_shap...]
where the time goes in v4:
time: 39.8 us; the launch traced here: 39.6 us
  Pallas kernels  38.9 us (98%)
  between operations  0.64 us (2%)
    pallas_call x1, Pallas kernels, on_device(): pl.pallas_call(functools.partial(kernel, (nz, nc, ntm, splits)), out_shap...  37.2 us
    pallas_call x1, Pallas kernels, on_device(): pl.pallas_call(write_out, out_shape=tuple((jax.ShapeDtypeStruct(o.shape,...  1.7 us

profile of v4, /device:TPU:3, one launch (start us, length us, event | category | flops | bytes accessed | tf_op | source)
XLA Modules:
  0.0 39.6 jit_solution(7965117645141567016)
XLA Ops:
  0.6 37.2 %shard_map.112 = (f32[64,1024]{1,0:T(8,128)}, f32[2,1024]{1,0:T(2,128)}, f32[2,1024]{1,0:T(2,128)}) custom-call(bf16[1024,2048]{1,0:T(8,128)(2,1)} %p_hbm.1, bf16[16,128]{1,0:T(8,128)(2,1)} %bitcast.8, s32[1,2048]{1,0:T(1,128)} %bitcast.6, s32[1,2048]{1,0:T(1,128)} %bitcast.7, bf16[256,512]{1,0:T(8,128)(2,1)} %shape_h.1, bf16[16,512]{1,0:T(8,128)(2,1)} %fshape_h.1, ...), custom_call_target="tpu_custom_call" | custom-call | tf_op jit(solution)/shard_map/pallas_call | solution.py:412
  37.9 1.7 %shard_map.113 = (f32[64,1024]{1,0:T(8,128)}, f32[2,1024]{1,0:T(2,128)}, f32[2,1024]{1,0:T(2,128)}) custom-call(f32[64,1024]{1,0:T(8,128)} %get-tuple-element.6.y, f32[2,1024]{1,0:T(2,128)} %get-tuple-element.7.fm, f32[2,1024]{1,0:T(2,128)} %get-tuple-element.8.fl), custom_call_target="tpu_custom_call" | custom-call | tf_op jit(solution)/shard_map/pallas_call | solution.py:464
